TPU v7x, 32 devices: a whole 2x2x4 slice. The times are simulated.
32 devices in a mesh: groups: 2 (over y), expert: 8 (over z, x), dp: 2 (over core).
Axes of the slice: x: 2, y: 2, z: 4, core: 2. Of those that a mesh axis runs over, the one named last changes fastest.
Arguments:
- tokens: bfloat16 [4096, 2048], P(('groups', 'expert', 'dp')), parts along dimension 0, may hold values from -6 to 6
- cotangent: bfloat16 [4096, 2048], P(('groups', 'expert', 'dp')), parts along dimension 0, may hold values from -6 to 6
- routes: int32 [4096, 4], P(('groups', 'expert', 'dp')), parts along dimension 0, may hold values from 0 to 15, as said below
- gates: float32 [4096, 4], P(('groups', 'expert', 'dp')), parts along dimension 0, may hold values from 0.05 to 0.6
- helper: int32 [32], P('groups'), parts along dimension 0, may hold values from 0 to 1
- w_gate: bfloat16 [16, 2048, 384], P(('expert', 'dp')), may hold values from -0.125 to 0.125
- w_up: bfloat16 [16, 2048, 384], P(('expert', 'dp')), may hold values from -0.125 to 0.125
- w_down: bfloat16 [16, 384, 2048], P(('expert', 'dp')), may hold values from -0.3125 to 0.3125
Outputs:
- grad_tokens: bfloat16 [4096, 2048], P(('groups', 'expert', 'dp')), parts along dimension 0
- grad_gate: bfloat16 [32, 2048, 384], P(('groups', 'expert', 'dp')), parts along dimension 0
- grad_up: bfloat16 [32, 2048, 384], P(('groups', 'expert', 'dp')), parts along dimension 0
- grad_down: bfloat16 [32, 384, 2048], P(('groups', 'expert', 'dp')), parts along dimension 0
There are 2 independent parts, one for each index of `groups`. A program takes and returns all parts, laid end to end along the dimension named above; an argument that names none is the same for every part. Nothing has to cross between parts.
Inputs may be any that keep to these rules, and one draw needn't show every extreme that they name: `routes`: each row names 4 different experts; the rows of one device name no expert more than 64 times, and some expert exactly 64 times in the rows of every device.
All inputs are finite; a program needn't handle non-finite values.
Results may differ from a plain program's by a relative error of at most 0.0065.
Values may be sent and summed in bfloat16 or wider, within the bound.
A program may use at most 128 MiB of HBM per device.

v0:
```python
import functools

import jax
import jax.numpy as jnp
from jax import lax
from jax.experimental import pallas as pl
from jax.experimental.pallas import tpu as pltpu
from jax.sharding import PartitionSpec as P

MESH = pl.DeviceIdType.MESH
BF16 = jnp.bfloat16
F32 = jnp.float32


def expert_pass(rows, scaled, gate_w, up_w, down_w):
    gate_pre = jnp.dot(rows, gate_w, preferred_element_type=jnp.float32)
    up_pre = jnp.dot(rows, up_w, preferred_element_type=jnp.float32)
    sigma = jax.nn.sigmoid(gate_pre)
    active = gate_pre * sigma
    hidden = (active * up_pre).astype(jnp.bfloat16)
    over_last = (((1,), (1,)), ((), ()))
    over_rows = (((0,), (0,)), ((), ()))
    back_hidden = lax.dot_general(scaled, down_w, over_last, preferred_element_type=jnp.float32)
    grad_gating = (back_hidden * up_pre * sigma * (1.0 + gate_pre * (1.0 - sigma))).astype(
        jnp.bfloat16
    )
    grad_upward = (back_hidden * active).astype(jnp.bfloat16)
    grad_down = lax.dot_general(hidden, scaled, over_rows, preferred_element_type=jnp.float32)
    grad_gate = lax.dot_general(rows, grad_gating, over_rows, preferred_element_type=jnp.float32)
    grad_up = lax.dot_general(rows, grad_upward, over_rows, preferred_element_type=jnp.float32)
    row_grads = lax.dot_general(grad_gating, gate_w, over_last, preferred_element_type=jnp.float32)
    row_grads = row_grads + lax.dot_general(
        grad_upward, up_w, over_last, preferred_element_type=jnp.float32
    )
    return (row_grads.astype(jnp.bfloat16), grad_gate, grad_up, grad_down)


def local(tokens, cotangent, routes, gates, helper, w_gate, w_up, w_down):
    tok_rows, width = tokens.shape
    top_count = routes.shape[1]
    devices = lax.axis_size(("expert", "dp"))
    route_cap = 2 * tok_rows * top_count // devices
    spill_cap = 3 * route_cap // 8
    home_cap = route_cap - spill_cap
    block_rows = tok_rows * top_count
    slots = devices * route_cap
    flat_ids = routes.reshape(block_rows)
    experts_row = jnp.arange(devices, dtype=jnp.int32)
    one_hot = (flat_ids[:, None] == experts_row[None, :]).astype(jnp.float32)
    positions = jnp.arange(block_rows, dtype=jnp.int32)
    lower = (positions[:, None] > positions[None, :]).astype(jnp.float32)
    before = jnp.dot(lower, one_hot, precision=lax.Precision.HIGHEST)
    route_rank = jnp.sum(before * one_hot, axis=1).astype(jnp.int32)
    partner_help = helper.reshape(devices // 2, 2)[:, ::-1].reshape(devices).astype(jnp.float32)
    helped = jnp.dot(one_hot, partner_help, precision=lax.Precision.HIGHEST) > 0.5
    spilled = route_rank >= home_cap
    kept = jnp.logical_not(spilled) | helped
    slot_index = jnp.where(kept, flat_ids * route_cap + route_rank, slots)
    source = jnp.full((slots + 1,), block_rows, jnp.int32).at[slot_index].set(positions)[:slots]
    token_of = jnp.where(source < block_rows, source // top_count, tok_rows)
    tokens_pad = jnp.concatenate([tokens, jnp.zeros((1, width), jnp.bfloat16)], axis=0)
    cot_pad = jnp.concatenate([cotangent, jnp.zeros((1, width), jnp.bfloat16)], axis=0)
    gate_pad = jnp.concatenate([gates.reshape(block_rows), jnp.zeros((1,), jnp.float32)], axis=0)
    send_rows = tokens_pad[token_of].reshape(devices, route_cap, width)
    send_scaled = (cot_pad[token_of].astype(jnp.float32) * gate_pad[source][:, None]).astype(
        jnp.bfloat16
    )
    send_scaled = send_scaled.reshape(devices, route_cap, width)
    recv_rows, recv_scaled = (
        lax.all_to_all(send_rows, ("expert", "dp"), split_axis=0, concat_axis=0, tiled=True),
        lax.all_to_all(send_scaled, ("expert", "dp"), split_axis=0, concat_axis=0, tiled=True),
    )
    gate_w = w_gate[0]
    up_w = w_up[0]
    down_w = w_down[0]
    whole_out = expert_pass(
        recv_rows.reshape(slots, width), recv_scaled.reshape(slots, width), gate_w, up_w, down_w
    )
    grad_gate = whole_out[1]
    grad_up = whole_out[2]
    grad_down = whole_out[3]
    row_grads = whole_out[0].reshape(devices, route_cap, width)
    back_rows = lax.all_to_all(row_grads, ("expert", "dp"), split_axis=0, concat_axis=0, tiled=True)
    back_pad = jnp.concatenate(
        [back_rows.reshape(slots, width), jnp.zeros((1, width), jnp.bfloat16)], axis=0
    )
    picked = back_pad[slot_index].reshape(tok_rows, top_count, width)
    grad_tokens = jnp.sum(picked.astype(jnp.float32), axis=1).astype(jnp.bfloat16)
    return (
        grad_tokens,
        grad_gate[None].astype(jnp.bfloat16),
        grad_up[None].astype(jnp.bfloat16),
        grad_down[None].astype(jnp.bfloat16),
    )


def ring_kernel(
    n, cap, home,
    tok_in, cot_in, rt_in, gt_in, help_in, wg_in, wu_in, wd_in,
    out_tok, out_gate, out_up, out_down,
    TOK, COT, RT, GT, HELP, WC, WD, R, S, H, GGU, PART, SIB, RB,
    lsem, wsem, ag_send, ag_recv, sib_send, sib_recv,
    ps_send, ps_recv, rs_send, rs_recv,
):
    half = n // 2
    rows, width = tok_in.shape
    hid = wd_in.shape[0]
    hr = rows // 2
    qr = rows // 4
    tile = width // 4
    e = lax.axis_index("expert")
    c = lax.axis_index("dp")
    z = e // 2
    x = e % 2
    pos = z + x * (n - 1 - 2 * z)

    def chip_at(q):
        q = q % n
        side = q // half
        return side * (2 * (n - 1 - q) + 1) + (1 - side) * 2 * q

    nxt = ({"expert": chip_at(pos + 1)}, {"expert": chip_at(pos + n - 1)})
    sib = {"dp": 1 - c}
    me = e * 2 + c

    def far(d):
        return pl.ds(d * hr, hr)

    local = [
        pltpu.make_async_copy(tok_in, TOK.at[0, 0], lsem.at[0]),
        pltpu.make_async_copy(cot_in, COT.at[0, 0], lsem.at[1]),
        pltpu.make_async_copy(rt_in, RT.at[0, 0], lsem.at[2]),
        pltpu.make_async_copy(gt_in, GT.at[0, 0], lsem.at[3]),
        pltpu.make_async_copy(help_in, HELP, lsem.at[4]),
    ]
    weights = [
        pltpu.make_async_copy(wg_in, WC.at[:, pl.ds(0, hid)], wsem.at[0]),
        pltpu.make_async_copy(wu_in, WC.at[:, pl.ds(hid, hid)], wsem.at[1]),
        pltpu.make_async_copy(wd_in, WD, wsem.at[2]),
    ]
    for cp in local + weights:
        cp.start()

    barrier = pltpu.get_barrier_semaphore()
    for who in (nxt[0], nxt[1], sib):
        pl.semaphore_signal(barrier, inc=1, device_id=who, device_id_type=MESH)
    pl.semaphore_wait(barrier, 3)

    bufs = (TOK, COT, RT, GT)
    own = (tok_in, cot_in, rt_in, gt_in)
    order = (2, 3, 0, 1)
    sends = []

    def put(src, dst, ssem, rsem, who):
        cp = pltpu.make_async_remote_copy(
            src_ref=src, dst_ref=dst, send_sem=ssem, recv_sem=rsem,
            device_id=who, device_id_type=MESH,
        )
        cp.start()
        sends.append(cp)

    def arrived(dst, ssem, rsem, who):
        pltpu.make_async_remote_copy(
            src_ref=dst, dst_ref=dst, send_sem=ssem, recv_sem=rsem,
            device_id=who, device_id_type=MESH,
        ).wait_recv()

    def slot(d, s):
        return (n - s) % n if d == 0 else s % n

    def piece(a, d, s):
        ref = bufs[a].at[slot(d, s), 0]
        if s == half and a < 2:
            return ref.at[far(d), :]
        return ref

    def sib_piece(a, d, s):
        ref = bufs[a].at[slot(d, s), 1]
        if s == half and a < 2:
            return ref.at[far(d), :]
        return ref

    def ring_put(a, d, s):
        if s == half and a >= 2 and d == 1:
            return
        src = own[a] if s == 1 else bufs[a].at[slot(d, s - 1), 0]
        if s == half and a < 2:
            src = src.at[far(d), :]
        put(src, piece(a, d, s), ag_send.at[a, d, s - 1], ag_recv.at[a, d, s - 1], nxt[d])

    def ring_take(a, d, s):
        if s == half and a >= 2 and d == 1:
            return
        arrived(piece(a, d, s), ag_send.at[a, d, s - 1], ag_recv.at[a, d, s - 1], nxt[d])
        if s < half:
            ring_put(a, d, s + 1)
        k = 1 + d * half + s - 1
        put(piece(a, d, s), sib_piece(a, d, s), sib_send.at[a, k], sib_recv.at[a, k], sib)

    def sib_take(a, d, s):
        if s == half and a >= 2 and d == 1:
            return
        k = 1 + d * half + s - 1
        arrived(sib_piece(a, d, s), sib_send.at[a, k], sib_recv.at[a, k], sib)

    for a in order:
        for d in (0, 1):
            ring_put(a, d, 1)
    for a in order:
        put(own[a], bufs[a].at[0, 1], sib_send.at[a, 0], sib_recv.at[a, 0], sib)

    earlier = (
        lax.broadcasted_iota(jnp.int32, (rows, rows), 0)
        < lax.broadcasted_iota(jnp.int32, (rows, rows), 1)
    ).astype(BF16)
    slot_ids = lax.broadcasted_iota(jnp.int32, (cap, rows), 0).astype(F32)
    over_last = (((1,), (1,)), ((), ()))
    over_rows = (((0,), (0,)), ((), ()))

    def token_part(blocks, base):
        partner = me + 1 - 2 * (me % 2)
        lanes = lax.broadcasted_iota(jnp.int32, HELP.shape, 1)
        flag = jnp.sum(jnp.where(lanes == partner, HELP[...], 0).astype(F32), axis=1, keepdims=True)
        limit = jnp.where(flag == 1.0, float(rows), home - 0.5)
        picks = []
        for i, (o, q) in enumerate(blocks):
            hit = RT[o, q] == me
            named = jnp.sum(hit.astype(F32), axis=0, keepdims=True)
            gate = jnp.sum(jnp.where(hit, GT[o, q], 0.0), axis=0, keepdims=True)
            named16 = jnp.broadcast_to(named, (16, rows)).astype(BF16)
            rank = jnp.dot(named16, earlier, preferred_element_type=F32)[0:1]
            kept = (named > 0.5) & (rank < limit)
            place = jnp.where(kept, rank, -1.0)
            hot = slot_ids == place
            gsel = jnp.sum(jnp.where(hot, gate, 0.0), axis=1, keepdims=True)
            hotf = hot.astype(F32)
            hotb = hotf.astype(BF16)
            picks.append((hotb, gsel, jnp.transpose(hotf).astype(BF16)))
            at = pl.ds(base + i * cap, cap)

            def gather(j, _, o=o, q=q, hotb=hotb, at=at):
                cols = pl.ds(pl.multiple_of(j * tile, tile), tile)
                R[at, cols] = jnp.dot(
                    hotb, TOK[o, q, :, cols], preferred_element_type=F32
                ).astype(BF16)
                return 0

            lax.fori_loop(0, width // tile, gather, 0)
        span = pl.ds(base, cap * len(blocks))
        pre = jnp.dot(R[span, :], WC[...], preferred_element_type=F32)
        return picks, pre

    def cot_part(blocks, base, picks, pre, leave):
        for i, (o, q) in enumerate(blocks):
            at = pl.ds(base + i * cap, cap)

            def gather(j, _, o=o, q=q, hotb=picks[i][0], gsel=picks[i][1], at=at):
                cols = pl.ds(pl.multiple_of(j * tile, tile), tile)
                S[at, cols] = (
                    gsel * jnp.dot(hotb, COT[o, q, :, cols], preferred_element_type=F32)
                ).astype(BF16)
                return 0

            lax.fori_loop(0, width // tile, gather, 0)
        span = pl.ds(base, cap * len(blocks))
        back = lax.dot_general(S[span, :], WD[...], over_last, preferred_element_type=F32)
        gate_pre = pre[:, :hid]
        up_pre = pre[:, hid:]
        sigma = jax.nn.sigmoid(gate_pre)
        active = gate_pre * sigma
        H[span, :] = (active * up_pre).astype(BF16)
        GGU[span, pl.ds(0, hid)] = (
            back * up_pre * sigma * (1.0 + gate_pre * (1.0 - sigma))
        ).astype(BF16)
        GGU[span, pl.ds(hid, hid)] = (back * active).astype(BF16)

        def spread(j, _):
            cols = pl.ds(pl.multiple_of(j * tile, tile), tile)
            grads = lax.dot_general(
                GGU[span, :], WC[cols, :], over_last, preferred_element_type=F32
            ).astype(BF16)
            for i, (o, q) in enumerate(blocks):
                PART[o, q, :, cols] = jnp.dot(
                    picks[i][2], grads[i * cap : (i + 1) * cap], preferred_element_type=F32
                ).astype(BF16)
            return 0

        for w in (0, 1):
            lax.fori_loop(2 * w, 2 * w + 2, spread, 0)
            leave(w)

    def part_put(o, w):
        cols = pl.ds(w * (width // 2), width // 2)
        put(
            PART.at[o, 1, :, cols], SIB.at[o, :, cols], ps_send.at[o, w], ps_recv.at[o, w], sib
        )

    def part_take(o):
        for w in (0, 1):
            cols = pl.ds(w * (width // 2), width // 2)
            arrived(SIB.at[o, :, cols], ps_send.at[o, w], ps_recv.at[o, w], sib)

    def sib_takes(arrays, s):
        for a in arrays:
            if s == 0:
                arrived(bufs[a].at[0, 1], sib_send.at[a, 0], sib_recv.at[a, 0], sib)
            else:
                for d in (0, 1):
                    sib_take(a, d, s)

    def blocks_of(s):
        if s == 0:
            return (0,), 0
        return ((n - s, s) if s < half else (half,)), 2 * cap + (s - 1) * 4 * cap

    def tokens_of(s):
        sib_takes((2, 3, 0), s)
        offs, base = blocks_of(s)
        return token_part([(o, q) for o in offs for q in (0, 1)], base)

    def rest_of(s, picks, pre):
        sib_takes((1,), s)
        offs, base = blocks_of(s)

        def leave(w):
            for o in offs:
                part_put(o, w)

        cot_part([(o, q) for o in offs for q in (0, 1)], base, picks, pre, leave)

    def batch(s):
        if s == 0:
            for cp in local + weights:
                cp.wait()
        rest_of(s, *tokens_of(s))

    for s in range(1, half):
        for a in (2, 3, 0):
            for d in (0, 1):
                ring_take(a, d, s)
        batch(s - 1)
        for d in (0, 1):
            ring_take(1, d, s)
    batch(half - 1)
    for a in (2, 3, 0):
        for d in (0, 1):
            ring_take(a, d, half)
    def rs_dst(d, j, h):
        return RB.at[d, j - 1, pl.ds(h * qr, qr), :]

    def rs_send_piece(d, j, h):
        k = half - j + 1
        o = k if d == 0 else n - k
        add = j > 2 or (j == 2 and h // 2 == d)
        if add:
            arrived(rs_dst(d, j - 1, h), rs_send.at[d, j - 2, h], rs_recv.at[d, j - 2, h], nxt[d])

        def add_rows(i, _):
            r = pl.ds(pl.multiple_of(h * qr + i * 16, 16), 16)
            total = PART[o, 0, r, :].astype(F32) + SIB[o, r, :].astype(F32)
            if add:
                total = total + RB[d, j - 2, r, :].astype(F32)
            PART[o, 0, r, :] = total.astype(BF16)
            return 0

        lax.fori_loop(0, qr // 16, add_rows, 0)
        put(
            PART.at[o, 0, pl.ds(h * qr, qr), :], rs_dst(d, j, h),
            rs_send.at[d, j - 1, h], rs_recv.at[d, j - 1, h], nxt[d],
        )

    def early(j):
        for h in (0, 1):
            for d in (0, 1):
                rs_send_piece(d, j, 2 * (1 - d) + h)

    def late(j):
        for h in (0, 1):
            for d in (0, 1):
                rs_send_piece(d, j, 2 * d + h)

    def down_grad():
        def body(j, _):
            cols = pl.ds(pl.multiple_of(j * tile, tile), tile)
            out_down[0, :, cols] = lax.dot_general(
                H[...], S[:, cols], over_rows, preferred_element_type=F32
            ).astype(BF16)
            return 0

        lax.fori_loop(0, width // tile, body, 0)

    wt = width // 8

    def in_grads(lo, hi):
        def body(j, _):
            cols = pl.ds(pl.multiple_of(j * wt, wt), wt)
            both = lax.dot_general(R[:, cols], GGU[...], over_rows, preferred_element_type=F32)
            out_gate[0, cols, :] = both[:, :hid].astype(BF16)
            out_up[0, cols, :] = both[:, hid:].astype(BF16)
            return 0

        lax.fori_loop(lo, hi, body, 0)

    for o in range(n):
        if o not in (0, half):
            part_take(o)
    early(2)
    last = tokens_of(half)
    for d in (0, 1):
        ring_take(1, d, half)
    rest_of(half, *last)
    early(3)
    part_take(half)
    late(1)
    down_grad()
    in_grads(0, 1)
    for j in range(2, half + 1):
        late(j)
        if j + 2 <= half:
            early(j + 2)
        lo = 1 + 7 * (j - 2) // (half - 1)
        in_grads(lo, 1 + 7 * (j - 1) // (half - 1))
    part_take(0)

    def landed(d, h):
        arrived(
            rs_dst(d, half, h), rs_send.at[d, half - 1, h], rs_recv.at[d, half - 1, h], nxt[d]
        )

    for d in (0, 1):
        for h in (0, 1):
            landed(d, 2 * (1 - d) + h)
    for h in (0, 1):
        for d in (0, 1):
            landed(d, 2 * d + h)

            def final(i, _, d=d, h=h):
                r = pl.ds(pl.multiple_of((2 * d + h) * qr + i * 16, 16), 16)
                total = PART[0, 0, r, :].astype(F32) + SIB[0, r, :].astype(F32)
                total = total + RB[0, half - 1, r, :].astype(F32)
                total = total + RB[1, half - 1, r, :].astype(F32)
                out_tok[r, :] = total.astype(BF16)
                return 0

            lax.fori_loop(0, qr // 16, final, 0)
    for cp in sends:
        cp.wait_send()


def gathered(tokens, cotangent, routes, gates, helper, w_gate, w_up, w_down):
    rows, width = tokens.shape
    n = lax.axis_size("expert")
    devices = n * lax.axis_size("dp")
    hid = w_gate.shape[2]
    cap = 2 * rows * routes.shape[1] // devices
    home = cap - 3 * cap // 8
    half = n // 2
    slots = devices * cap
    top = routes.shape[1]
    anyw = pl.BlockSpec(memory_space=pl.ANY)
    vmem = pl.BlockSpec(memory_space=pltpu.VMEM)
    dma = pltpu.SemaphoreType.DMA
    return pl.pallas_call(
        functools.partial(ring_kernel, n, cap, home),
        out_shape=(
            pltpu.VMEM((rows, width), BF16),
            pltpu.VMEM((1, width, hid), BF16),
            pltpu.VMEM((1, width, hid), BF16),
            pltpu.VMEM((1, hid, width), BF16),
        ),
        in_specs=[anyw] * 8,
        out_specs=(vmem, vmem, vmem, vmem),
        scratch_shapes=[
            pltpu.VMEM((n, 2, rows, width), BF16),
            pltpu.VMEM((n, 2, rows, width), BF16),
            pltpu.VMEM((n, 2, top, rows), jnp.int32),
            pltpu.VMEM((n, 2, top, rows), F32),
            pltpu.VMEM((1, devices), jnp.int32),
            pltpu.VMEM((width, 2 * hid), BF16),
            pltpu.VMEM((hid, width), BF16),
            pltpu.VMEM((slots, width), BF16),
            pltpu.VMEM((slots, width), BF16),
            pltpu.VMEM((slots, hid), BF16),
            pltpu.VMEM((slots, 2 * hid), BF16),
            pltpu.VMEM((n, 2, rows, width), BF16),
            pltpu.VMEM((n, rows, width), BF16),
            pltpu.VMEM((2, half, rows, width), BF16),
            dma((5,)),
            dma((3,)),
            dma((4, 2, half)),
            dma((4, 2, half)),
            dma((4, 2 * half + 1)),
            dma((4, 2 * half + 1)),
            dma((n, 2)),
            dma((n, 2)),
            dma((2, half, 4)),
            dma((2, half, 4)),
        ],
        compiler_params=pltpu.CompilerParams(
            collective_id=0, has_side_effects=True, vmem_limit_bytes=56 * 1024 * 1024
        ),
    )(tokens, cotangent, routes.T, gates.T, helper[None], w_gate[0], w_up[0], w_down[0])


def plan(tokens, cotangent, routes, *rest):
    rows = tokens.shape[0]
    n, cores = lax.axis_size("expert"), lax.axis_size("dp")
    slots = 2 * rows * routes.shape[1]
    few = cores == 2 and n % 2 == 0 and n >= 6 and rows % 64 == 0 and n * cores * rows <= 2 * slots
    return (gathered if few else local)(tokens, cotangent, routes, *rest)


def solution(mesh):
    return jax.shard_map(
        plan,
        mesh=mesh,
        in_specs=(
            P(("groups", "expert", "dp"), None),
            P(("groups", "expert", "dp"), None),
            P(("groups", "expert", "dp"), None),
            P(("groups", "expert", "dp"), None),
            P("groups"),
            P(("expert", "dp"), None, None),
            P(("expert", "dp"), None, None),
            P(("expert", "dp"), None, None),
        ),
        out_specs=(
            P(("groups", "expert", "dp"), None),
            P(("groups", "expert", "dp"), None, None),
            P(("groups", "expert", "dp"), None, None),
            P(("groups", "expert", "dp"), None, None),
        ),
        check_vma=False,
    )
```

profile of v0, /device:TPU:0, one launch (start us, length us, event | category | flops | bytes accessed | tf_op | source)
XLA Modules:
  0.0 137.9 jit_solution(489032248298195529)
XLA Ops:
  0.6 133.0 %shard_map.111 = (bf16[128,2048]{1,0:T(8,128)(2,1)S(1)}, bf16[1,2048,384]{2,1,0:T(8,128)(2,1)S(1)}, bf16[1,2048,384]{2,1,0:T(8,128)(2,1)S(1)}, bf16[1,384,2048]{2,1,0:T(8,128)(2,1)S(1)}) custom-call(bf16[128,2048]{1,0:T(8,128)(2,1)} %tok_in.1, bf16[128,2048]{1,0:T(8,128)(2,1)} %cot_in.1, s32[4,128]{1,0:T(4,128)} %bitcast.9, f32[4,128]{1,0:T(4,128)} %bitcast.10, ...), custom_call_target="tpu_custom_call" | custom-call | tf_op jit(solution)/shard_map/pallas_call | solution.py:463
  133.7 0.8 copy.16
  134.5 1.1 copy.17
  135.6 1.1 copy.18
  136.8 1.1 copy.19
where the time goes:
time: 138 us
  Pallas kernels  133 us (96%)
  local copies, waits for them, and re-layouts  4.22 us (3%)
    pallas_call x1, Pallas kernels, gathered(): pl.pallas_call(functools.partial(ring_kernel, n, cap, home), out_shape=(p...  133 us
    unnamed x4, local copies, waits for them, and re-layouts  4.22 us

commit v1 on v0

--- a/solution.py
+++ b/solution.py
@@ -502,12 +502,37 @@
     )(tokens, cotangent, routes.T, gates.T, helper[None], w_gate[0], w_up[0], w_down[0])
 
 
+def flush_kernel(*refs):
+    count = len(refs) // 2
+    sems = refs[-1]
+    copies = [
+        pltpu.make_async_copy(refs[i], refs[count + i], sems.at[i]) for i in range(count)
+    ]
+    for cp in copies:
+        cp.start()
+    for cp in copies:
+        cp.wait()
+
+
+def flush(*arrays):
+    return pl.pallas_call(
+        flush_kernel,
+        out_shape=tuple(jax.ShapeDtypeStruct(a.shape, a.dtype) for a in arrays),
+        in_specs=[pl.BlockSpec(memory_space=pltpu.VMEM)] * len(arrays),
+        out_specs=tuple(pl.BlockSpec(memory_space=pl.ANY) for _ in arrays),
+        scratch_shapes=[pltpu.SemaphoreType.DMA((len(arrays),))],
+        compiler_params=pltpu.CompilerParams(vmem_limit_bytes=1024 * 1024),
+    )(*arrays)
+
+
 def plan(tokens, cotangent, routes, *rest):
     rows = tokens.shape[0]
     n, cores = lax.axis_size("expert"), lax.axis_size("dp")
     slots = 2 * rows * routes.shape[1]
     few = cores == 2 and n % 2 == 0 and n >= 6 and rows % 64 == 0 and n * cores * rows <= 2 * slots
-    return (gathered if few else local)(tokens, cotangent, routes, *rest)
+    if few:
+        return flush(*gathered(tokens, cotangent, routes, *rest))
+    return local(tokens, cotangent, routes, *rest)
 
 
 def solution(mesh):

time: 138 us -> 136 us (0.986)
  local copies, waits for them, and re-layouts: 4.22 us -> 0 us
  Pallas kernels: 133 us -> 135 us
    unnamed x4 -> x0, local copies, waits for them, and re-layouts: 4.22 us -> none
    pallas_call x0 -> x1, Pallas kernels: none -> 2.39 us  [flush(): pl.pallas_call(flush_kernel, out_shape=tuple((jax.ShapeDtypeStruct(a.shap...]
where the time goes in v1:
time: 136 us
  Pallas kernels  135 us (99%)
    pallas_call x1, Pallas kernels, gathered(): pl.pallas_call(functools.partial(ring_kernel, n, cap, home), out_shape=(p...  133 us

profile of v1, /device:TPU:0, one launch (start us, length us, event | category | flops | bytes accessed | tf_op | source)
XLA Modules:
  0.0 136.2 jit_solution(7246877732160202698)
XLA Ops:
  0.6 133.0 %shard_map.111 = (bf16[128,2048]{1,0:T(8,128)(2,1)S(1)}, bf16[1,2048,384]{2,1,0:T(8,128)(2,1)S(1)}, bf16[1,2048,384]{2,1,0:T(8,128)(2,1)S(1)}, bf16[1,384,2048]{2,1,0:T(8,128)(2,1)S(1)}) custom-call(bf16[128,2048]{1,0:T(8,128)(2,1)} %tok_in.1, bf16[128,2048]{1,0:T(8,128)(2,1)} %cot_in.1, s32[4,128]{1,0:T(4,128)} %bitcast.9, f32[4,128]{1,0:T(4,128)} %bitcast.10, ...), custom_call_target="tpu_custom_call" | custom-call | tf_op jit(solution)/shard_map/pallas_call | solution.py:463
  133.7 2.4 %shard_map.112 = (bf16[128,2048]{1,0:T(8,128)(2,1)}, bf16[1,2048,384]{2,1,0:T(8,128)(2,1)}, bf16[1,2048,384]{2,1,0:T(8,128)(2,1)}, bf16[1,384,2048]{2,1,0:T(8,128)(2,1)}) custom-call(bf16[128,2048]{1,0:T(8,128)(2,1)S(1)} %get-tuple-element.8.refs_0_, bf16[1,2048,384]{2,1,0:T(8,128)(2,1)S(1)} %get-tuple-element.9.refs_1_, ...), custom_call_target="tpu_custom_call" | custom-call | tf_op jit(solution)/shard_map/pallas_call | solution.py:518

commit v2 on v1

--- a/solution.py
+++ b/solution.py
@@ -106,7 +106,7 @@
     rows, width = tok_in.shape
     hid = wd_in.shape[0]
     hr = rows // 2
-    qr = rows // 4
+    hw = width // 2
     tile = width // 4
     e = lax.axis_index("expert")
     c = lax.axis_index("dp")
@@ -295,8 +295,8 @@
             PART.at[o, 1, :, cols], SIB.at[o, :, cols], ps_send.at[o, w], ps_recv.at[o, w], sib
         )
 
-    def part_take(o):
-        for w in (0, 1):
+    def part_take(o, halves=(0, 1)):
+        for w in halves:
             cols = pl.ds(w * (width // 2), width // 2)
             arrived(SIB.at[o, :, cols], ps_send.at[o, w], ps_recv.at[o, w], sib)
 
@@ -334,19 +334,23 @@
                 cp.wait()
         rest_of(s, *tokens_of(s))
 
+    for cp in local + weights:
+        cp.wait()
+    rest_of(0, *tokens_of(0))
     for s in range(1, half):
         for a in (2, 3, 0):
             for d in (0, 1):
                 ring_take(a, d, s)
-        batch(s - 1)
+        ready = tokens_of(s)
         for d in (0, 1):
             ring_take(1, d, s)
-    batch(half - 1)
+        rest_of(s, *ready)
     for a in (2, 3, 0):
         for d in (0, 1):
             ring_take(a, d, half)
+
     def rs_dst(d, j, h):
-        return RB.at[d, j - 1, pl.ds(h * qr, qr), :]
+        return RB.at[d, j - 1, pl.ds(h // 2 * hr, hr), pl.ds(h % 2 * hw, hw)]
 
     def rs_send_piece(d, j, h):
         k = half - j + 1
@@ -355,17 +359,19 @@
         if add:
             arrived(rs_dst(d, j - 1, h), rs_send.at[d, j - 2, h], rs_recv.at[d, j - 2, h], nxt[d])
 
+        cols = pl.ds(h % 2 * hw, hw)
+
         def add_rows(i, _):
-            r = pl.ds(pl.multiple_of(h * qr + i * 16, 16), 16)
-            total = PART[o, 0, r, :].astype(F32) + SIB[o, r, :].astype(F32)
+            r = pl.ds(pl.multiple_of(h // 2 * hr + i * 16, 16), 16)
+            total = PART[o, 0, r, cols].astype(F32) + SIB[o, r, cols].astype(F32)
             if add:
-                total = total + RB[d, j - 2, r, :].astype(F32)
-            PART[o, 0, r, :] = total.astype(BF16)
+                total = total + RB[d, j - 2, r, cols].astype(F32)
+            PART[o, 0, r, cols] = total.astype(BF16)
             return 0
 
-        lax.fori_loop(0, qr // 16, add_rows, 0)
+        lax.fori_loop(0, hr // 16, add_rows, 0)
         put(
-            PART.at[o, 0, pl.ds(h * qr, qr), :], rs_dst(d, j, h),
+            PART.at[o, 0, pl.ds(h // 2 * hr, hr), cols], rs_dst(d, j, h),
             rs_send.at[d, j - 1, h], rs_recv.at[d, j - 1, h], nxt[d],
         )
 
@@ -410,8 +416,10 @@
         ring_take(1, d, half)
     rest_of(half, *last)
     early(3)
-    part_take(half)
-    late(1)
+    for h in (0, 1):
+        part_take(half, (h,))
+        for d in (0, 1):
+            rs_send_piece(d, 1, 2 * d + h)
     down_grad()
     in_grads(0, 1)
     for j in range(2, half + 1):
@@ -435,14 +443,15 @@
             landed(d, 2 * d + h)
 
             def final(i, _, d=d, h=h):
-                r = pl.ds(pl.multiple_of((2 * d + h) * qr + i * 16, 16), 16)
-                total = PART[0, 0, r, :].astype(F32) + SIB[0, r, :].astype(F32)
-                total = total + RB[0, half - 1, r, :].astype(F32)
-                total = total + RB[1, half - 1, r, :].astype(F32)
-                out_tok[r, :] = total.astype(BF16)
+                cols = pl.ds(h * hw, hw)
+                r = pl.ds(pl.multiple_of(d * hr + i * 16, 16), 16)
+                total = PART[0, 0, r, cols].astype(F32) + SIB[0, r, cols].astype(F32)
+                total = total + RB[0, half - 1, r, cols].astype(F32)
+                total = total + RB[1, half - 1, r, cols].astype(F32)
+                out_tok[r, cols] = total.astype(BF16)
                 return 0
 
-            lax.fori_loop(0, qr // 16, final, 0)
+            lax.fori_loop(0, hr // 16, final, 0)
     for cp in sends:
         cp.wait_send()
 
@@ -505,9 +514,16 @@
 def flush_kernel(*refs):
     count = len(refs) // 2
     sems = refs[-1]
-    copies = [
-        pltpu.make_async_copy(refs[i], refs[count + i], sems.at[i]) for i in range(count)
-    ]
+    copies = []
+    for i in range(count):
+        rows = refs[i].shape[-2]
+        parts = 4 if rows % 64 == 0 else 1
+        for k in range(parts):
+            at = pl.ds(k * (rows // parts), rows // parts)
+            at = (at,) if len(refs[i].shape) == 2 else (0, at)
+            copies.append(
+                pltpu.make_async_copy(refs[i].at[at], refs[count + i].at[at], sems.at[i, k])
+            )
     for cp in copies:
         cp.start()
     for cp in copies:
@@ -520,7 +536,7 @@
         out_shape=tuple(jax.ShapeDtypeStruct(a.shape, a.dtype) for a in arrays),
         in_specs=[pl.BlockSpec(memory_space=pltpu.VMEM)] * len(arrays),
         out_specs=tuple(pl.BlockSpec(memory_space=pl.ANY) for _ in arrays),
-        scratch_shapes=[pltpu.SemaphoreType.DMA((len(arrays),))],
+        scratch_shapes=[pltpu.SemaphoreType.DMA((len(arrays), 4))],
         compiler_params=pltpu.CompilerParams(vmem_limit_bytes=1024 * 1024),
     )(*arrays)
 

time: 136 us -> 133 us (0.978)
  Pallas kernels: 135 us -> 132 us
    pallas_call x1, Pallas kernels: 133 us -> 129 us  [gathered(): pl.pallas_call(functools.partial(ring_kernel, n, cap, home), out_shape=(p...]
where the time goes in v2:
time: 133 us
  Pallas kernels  132 us (99%)
    pallas_call x1, Pallas kernels, gathered(): pl.pallas_call(functools.partial(ring_kernel, n, cap, home), out_shape=(p...  129 us

profile of v2, /device:TPU:0, one launch (start us, length us, event | category | flops | bytes accessed | tf_op | source)
XLA Modules:
  0.0 132.7 jit_solution(10016419693577450693)
XLA Ops:
  0.6 129.4 %shard_map.111 = (bf16[128,2048]{1,0:T(8,128)(2,1)S(1)}, bf16[1,2048,384]{2,1,0:T(8,128)(2,1)S(1)}, bf16[1,2048,384]{2,1,0:T(8,128)(2,1)S(1)}, bf16[1,384,2048]{2,1,0:T(8,128)(2,1)S(1)}) custom-call(bf16[128,2048]{1,0:T(8,128)(2,1)} %tok_in.1, bf16[128,2048]{1,0:T(8,128)(2,1)} %cot_in.1, s32[4,128]{1,0:T(4,128)} %bitcast.9, f32[4,128]{1,0:T(4,128)} %bitcast.10, ...), custom_call_target="tpu_custom_call" | custom-call | tf_op jit(solution)/shard_map/pallas_call | solution.py:472
  130.0 2.5 %shard_map.112 = (bf16[128,2048]{1,0:T(8,128)(2,1)}, bf16[1,2048,384]{2,1,0:T(8,128)(2,1)}, bf16[1,2048,384]{2,1,0:T(8,128)(2,1)}, bf16[1,384,2048]{2,1,0:T(8,128)(2,1)}) custom-call(bf16[128,2048]{1,0:T(8,128)(2,1)S(1)} %get-tuple-element.8.refs_0_, bf16[1,2048,384]{2,1,0:T(8,128)(2,1)S(1)} %get-tuple-element.9.refs_1_, ...), custom_call_target="tpu_custom_call" | custom-call | tf_op jit(solution)/shard_map/pallas_call | solution.py:534

commit v3 on v2

--- a/solution.py
+++ b/solution.py
@@ -251,17 +251,16 @@
         return picks, pre
 
     def cot_part(blocks, base, picks, pre, leave):
-        for i, (o, q) in enumerate(blocks):
-            at = pl.ds(base + i * cap, cap)
-
-            def gather(j, _, o=o, q=q, hotb=picks[i][0], gsel=picks[i][1], at=at):
-                cols = pl.ds(pl.multiple_of(j * tile, tile), tile)
-                S[at, cols] = (
-                    gsel * jnp.dot(hotb, COT[o, q, :, cols], preferred_element_type=F32)
+        def gather(j, _):
+            cols = pl.ds(pl.multiple_of(j * tile, tile), tile)
+            for i, (o, q) in enumerate(blocks):
+                S[pl.ds(base + i * cap, cap), cols] = (
+                    picks[i][1]
+                    * jnp.dot(picks[i][0], COT[o, q, :, cols], preferred_element_type=F32)
                 ).astype(BF16)
-                return 0
-
-            lax.fori_loop(0, width // tile, gather, 0)
+            return 0
+
+        lax.fori_loop(0, width // tile, gather, 0)
         span = pl.ds(base, cap * len(blocks))
         back = lax.dot_general(S[span, :], WD[...], over_last, preferred_element_type=F32)
         gate_pre = pre[:, :hid]
@@ -318,13 +317,15 @@
         offs, base = blocks_of(s)
         return token_part([(o, q) for o in offs for q in (0, 1)], base)
 
-    def rest_of(s, picks, pre):
+    def rest_of(s, picks, pre, between=None):
         sib_takes((1,), s)
         offs, base = blocks_of(s)
 
         def leave(w):
             for o in offs:
                 part_put(o, w)
+            if between is not None and w == 0:
+                between()
 
         cot_part([(o, q) for o in offs for q in (0, 1)], base, picks, pre, leave)
 
@@ -375,10 +376,13 @@
             rs_send.at[d, j - 1, h], rs_recv.at[d, j - 1, h], nxt[d],
         )
 
+    def early_half(j, h):
+        for d in (0, 1):
+            rs_send_piece(d, j, 2 * (1 - d) + h)
+
     def early(j):
         for h in (0, 1):
-            for d in (0, 1):
-                rs_send_piece(d, j, 2 * (1 - d) + h)
+            early_half(j, h)
 
     def late(j):
         for h in (0, 1):
@@ -414,8 +418,8 @@
     last = tokens_of(half)
     for d in (0, 1):
         ring_take(1, d, half)
-    rest_of(half, *last)
-    early(3)
+    rest_of(half, *last, functools.partial(early_half, 3, 0))
+    early_half(3, 1)
     for h in (0, 1):
         part_take(half, (h,))
         for d in (0, 1):

time: 133 us -> 131 us (0.985)
  Pallas kernels: 132 us -> 130 us
    pallas_call x1, Pallas kernels: 129 us -> 127 us  [gathered(): pl.pallas_call(functools.partial(ring_kernel, n, cap, home), out_shape=(p...]
where the time goes in v3:
time: 131 us; the launch traced here: 130 us
  Pallas kernels  130 us (99%)
    pallas_call x1, Pallas kernels, gathered(): pl.pallas_call(functools.partial(ring_kernel, n, cap, home), out_shape=(p...  127 us

profile of v3, /device:TPU:0, one launch (start us, length us, event | category | flops | bytes accessed | tf_op | source)
XLA Modules:
  0.0 130.4 jit_solution(17439259041416567129)
XLA Ops:
  0.6 127.2 %shard_map.111 = (bf16[128,2048]{1,0:T(8,128)(2,1)S(1)}, bf16[1,2048,384]{2,1,0:T(8,128)(2,1)S(1)}, bf16[1,2048,384]{2,1,0:T(8,128)(2,1)S(1)}, bf16[1,384,2048]{2,1,0:T(8,128)(2,1)S(1)}) custom-call(bf16[128,2048]{1,0:T(8,128)(2,1)} %tok_in.1, bf16[128,2048]{1,0:T(8,128)(2,1)} %cot_in.1, s32[4,128]{1,0:T(4,128)} %bitcast.9, f32[4,128]{1,0:T(4,128)} %bitcast.10, ...), custom_call_target="tpu_custom_call" | custom-call | tf_op jit(solution)/shard_map/pallas_call | solution.py:476
  127.8 2.5 %shard_map.112 = (bf16[128,2048]{1,0:T(8,128)(2,1)}, bf16[1,2048,384]{2,1,0:T(8,128)(2,1)}, bf16[1,2048,384]{2,1,0:T(8,128)(2,1)}, bf16[1,384,2048]{2,1,0:T(8,128)(2,1)}) custom-call(bf16[128,2048]{1,0:T(8,128)(2,1)S(1)} %get-tuple-element.8.refs_0_, bf16[1,2048,384]{2,1,0:T(8,128)(2,1)S(1)} %get-tuple-element.9.refs_1_, ...), custom_call_target="tpu_custom_call" | custom-call | tf_op jit(solution)/shard_map/pallas_call | solution.py:538
